TPU v7x, 256 devices: a whole 4x4x8 slice. The times are simulated.
256 devices in a mesh: ctx: 64 (over z, x, core), dp: 4 (over y).
Axes of the slice: x: 4, y: 4, z: 8, core: 2. Of those that a mesh axis runs over, the one named last changes fastest.
Arguments:
- query_policy: bfloat16 [4, 2, 8192, 2048], P('dp', None, 'ctx'), may hold values from -6 to 6
- key_policy: bfloat16 [4, 2, 8192, 512], P('dp', None, 'ctx'), may hold values from -6 to 6
- value_policy: bfloat16 [4, 2, 8192, 512], P('dp', None, 'ctx'), may hold values from -60 to 60
- query_reference: bfloat16 [4, 2, 8192, 2048], P('dp', None, 'ctx'), may hold values from -6 to 6
- key_reference: bfloat16 [4, 2, 8192, 512], P('dp', None, 'ctx'), may hold values from -6 to 6
- value_reference: bfloat16 [4, 2, 8192, 512], P('dp', None, 'ctx'), may hold values from -60 to 60
- readout: bfloat16 [4, 2, 8192, 2048], P('dp', None, 'ctx'), may hold values from -0.0029296875 to 0.0029296875
- response_mask: int32 [4, 2, 8192], P('dp', None, 'ctx'), may hold values from 0 to 1, as said below
Outputs:
- query_gradient_rows: bfloat16 [4, 2, 8192, 2048], P('dp', None, 'ctx')
- key_gradient_rows: bfloat16 [4, 2, 8192, 512], P('dp', None, 'ctx')
- value_gradient_rows: bfloat16 [4, 2, 8192, 512], P('dp', None, 'ctx')
- pair_loss: float32 [], replicated
Inputs may be any that keep to these rules, and one draw needn't show every extreme that they name: `response_mask`: in each pair the mask is 1 exactly from the prompt's end (1 to 2048, the same for both sequences) up to but excluding the sequence's own end (4096 to 8192).
All inputs are finite; a program needn't handle non-finite values.
Results may differ from a plain program's by a relative error of at most 0.018.
Values may be sent and summed in bfloat16 or wider, within the bound.
No kernel may reach another device: no remote copies, remote signals or barrier semaphores. Data moves between devices by JAX's collectives and lax.ppermute only.
A program may use at most 192 MiB of HBM per device.

v0:
```python
import math
import jax
import jax.numpy as jnp
from jax import lax
from jax.sharding import PartitionSpec as P

HEADS = 16
KV_HEADS = 4
D_HEAD = 128
dpo_beta = 0.5
epsilon = 1e-06


def carried_in(x, axis, join, neutral, backward):
    count = lax.axis_size(axis)
    place = lax.axis_index(axis)
    ahead = count - 1 - place if backward else place
    gathered = lax.all_gather(x.astype(jnp.bfloat16), axis)
    state = jnp.zeros_like(x) + jnp.asarray(neutral, x.dtype)

    def one(turn, state):
        source = count - 1 - turn if backward else turn
        return join(state, lax.dynamic_index_in_dim(gathered, source, 0, False).astype(x.dtype))

    return lax.fori_loop(0, ahead, one, state)


def add_states(earlier, following):
    return earlier + following


def causal_mask(block_rows):
    positions = jnp.arange(block_rows)
    return positions[:, None] >= positions[None, :]


def span_state(key_head_rows, value_head_rows):
    return jnp.einsum(
        "asgd,asge->agde", key_head_rows, value_head_rows, preferred_element_type=jnp.float32
    )


def span_forward(query_head_rows, key_head_rows, value_head_rows, carried):
    causal = causal_mask(query_head_rows.shape[1])
    pair_score_rows = jnp.einsum(
        "atgrd,asgd->agrts", query_head_rows, key_head_rows, preferred_element_type=jnp.float32
    )
    pair_score_rows = jnp.where(causal, pair_score_rows, 0.0).astype(jnp.bfloat16)
    carried_low = carried.astype(jnp.bfloat16)
    unnormed_output = jnp.einsum(
        "agrts,asgd->atgrd", pair_score_rows, value_head_rows, preferred_element_type=jnp.float32
    )
    unnormed_output = unnormed_output + jnp.einsum(
        "atgrd,agde->atgre", query_head_rows, carried_low, preferred_element_type=jnp.float32
    )
    inverse = lax.rsqrt(
        jnp.mean(unnormed_output * unnormed_output, axis=-1, keepdims=True) + epsilon
    )
    return (pair_score_rows, carried_low, unnormed_output * inverse, inverse)


def shards(
    query_policy,
    key_policy,
    value_policy,
    query_reference,
    key_reference,
    value_reference,
    readout,
    response_mask,
):
    block_rows = query_policy.shape[2]
    per_group = HEADS // KV_HEADS

    def split_query(array):
        return array.reshape(2, block_rows, KV_HEADS, per_group, D_HEAD)

    def split_shared(array):
        return array.reshape(2, block_rows, KV_HEADS, D_HEAD)

    query_pol = split_query(query_policy)
    key_pol = split_shared(key_policy)
    value_pol = split_shared(value_policy)
    query_ref = split_query(query_reference)
    key_ref = split_shared(key_reference)
    value_ref = split_shared(value_reference)
    states_policy = span_state(key_pol, value_pol)
    states_reference = span_state(key_ref, value_ref)
    carried_policy = carried_in(
        states_policy, "ctx", add_states, jnp.zeros_like(states_policy), False
    )
    carried_reference = carried_in(
        states_reference, "ctx", add_states, jnp.zeros_like(states_reference), False
    )
    scores_policy, carried_policy_low, normed_policy, inverse_policy = span_forward(
        query_pol, key_pol, value_pol, carried_policy
    )
    normed_reference = span_forward(query_ref, key_ref, value_ref, carried_reference)[2]
    read_heads = split_query(readout)
    mask_rows = response_mask.reshape(2, block_rows).astype(jnp.float32)
    policy_tokens = jnp.sum(normed_policy * read_heads, axis=(2, 3, 4))
    reference_tokens = jnp.sum(normed_reference * read_heads, axis=(2, 3, 4))
    sums = jnp.stack(
        [jnp.sum(mask_rows * policy_tokens, axis=1), jnp.sum(mask_rows * reference_tokens, axis=1)]
    )
    totals = lax.psum(sums, "ctx")
    delta = totals[0, 0] - totals[0, 1] - (totals[1, 0] - totals[1, 1])
    pair_loss = lax.psum(jax.nn.softplus(-dpo_beta * delta), "dp") / lax.axis_size("dp")
    scale = math.sqrt(HEADS * D_HEAD * block_rows * lax.axis_size("ctx"))
    pull = dpo_beta * jax.nn.sigmoid(-dpo_beta * delta) * scale
    weights = jnp.stack([-pull, pull])
    upstream = (weights[:, None] * mask_rows)[:, :, None, None, None] * read_heads
    pulled_back_state = upstream - normed_policy * jnp.mean(
        upstream * normed_policy, axis=-1, keepdims=True
    )
    pulled_back_state = (pulled_back_state * inverse_policy).astype(jnp.bfloat16)
    block_grad = jnp.einsum(
        "atgrd,atgre->agde", query_pol, pulled_back_state, preferred_element_type=jnp.float32
    )
    later = carried_in(block_grad, "ctx", add_states, jnp.zeros_like(block_grad), True)
    later_low = later.astype(jnp.bfloat16)
    causal = causal_mask(block_rows)
    score_gradient = jnp.einsum(
        "atgre,asge->agrts", pulled_back_state, value_pol, preferred_element_type=jnp.float32
    )
    score_gradient = jnp.where(causal, score_gradient, 0.0).astype(jnp.bfloat16)
    query_gradient_rows = jnp.einsum(
        "agrts,asgd->atgrd", score_gradient, key_pol, preferred_element_type=jnp.float32
    )
    query_gradient_rows = query_gradient_rows + jnp.einsum(
        "atgre,agde->atgrd",
        pulled_back_state,
        carried_policy_low,
        preferred_element_type=jnp.float32,
    )
    key_gradient_rows = jnp.einsum(
        "agrts,atgrd->asgd", score_gradient, query_pol, preferred_element_type=jnp.float32
    )
    key_gradient_rows = key_gradient_rows + jnp.einsum(
        "asge,agde->asgd", value_pol, later_low, preferred_element_type=jnp.float32
    )
    value_gradient_rows = jnp.einsum(
        "agrts,atgre->asge", scores_policy, pulled_back_state, preferred_element_type=jnp.float32
    )
    value_gradient_rows = value_gradient_rows + jnp.einsum(
        "asgd,agde->asge", key_pol, later_low, preferred_element_type=jnp.float32
    )
    return (
        query_gradient_rows.reshape(1, 2, block_rows, HEADS * D_HEAD).astype(jnp.bfloat16),
        key_gradient_rows.reshape(1, 2, block_rows, KV_HEADS * D_HEAD).astype(jnp.bfloat16),
        value_gradient_rows.reshape(1, 2, block_rows, KV_HEADS * D_HEAD).astype(jnp.bfloat16),
        pair_loss,
    )


def solution(mesh):
    placed = (
        P("dp", None, "ctx", None),
        P("dp", None, "ctx", None),
        P("dp", None, "ctx", None),
        P("dp", None, "ctx", None),
        P("dp", None, "ctx", None),
        P("dp", None, "ctx", None),
        P("dp", None, "ctx", None),
        P("dp", None, "ctx"),
    )
    return jax.shard_map(
        shards,
        mesh=mesh,
        in_specs=placed,
        out_specs=(
            P("dp", None, "ctx", None),
            P("dp", None, "ctx", None),
            P("dp", None, "ctx", None),
            P(),
        ),
        check_vma=False,
    )
```

profile of v0, /device:TPU:1, one launch (start us, length us, event | category | flops | bytes accessed | tf_op | source)
XLA Modules:
  0.0 600.7 jit_solution(8161237302858355317)
XLA Ops:
  8.3 1.1 reshape.127
  13.5 2.0 reshape.129
  15.5 3.0 copy.51
  18.5 1.5 fusion.2
  20.1 95.2 %all-gather.7.cloned.1.call-done = bf16[128,4,128,128]{3,2,1,0:T(8,128)(2,1)} async-done(((bf16[2,4,128,128]{3,2,1,0:T(8,128)(2,1)}), bf16[128,4,128,128]{3,2,1,0:T(8,128)(2,1)}) %all-gather.7.cloned.1.call-update) | async-done | bytes 16777232 | tf_op jit(solution)/shard_map/all_gather | solution.py:18
  115.3 1.1 while.32
  115.4 1.1 convert_add_fusion.6
  116.5 1.8 fusion.18
  118.3 97.1 %all-gather.9.cloned.1.call-done = bf16[128,4,128,128]{3,2,1,0:T(8,128)(2,1)} async-done(((bf16[2,4,128,128]{3,2,1,0:T(8,128)(2,1)}), bf16[128,4,128,128]{3,2,1,0:T(8,128)(2,1)}) %all-gather.9.cloned.1.call-update) | async-done | bytes 16777232 | tf_op jit(solution)/shard_map/all_gather | solution.py:18
  215.4 1.1 while.33
  216.6 1.8 fusion.13
  219.7 4.1 multiply_reduce_fusion.2
  223.8 2.8 multiply_reduce_fusion.3
  226.8 188.1 %psum.14 = f32[2,2]{1,0:T(2,128)S(1)} all-reduce(f32[2,2]{1,0:T(2,128)S(1)} %pad_maximum_fusion), channel_id=1, replica_groups=mesh['ctx'=64,'dp'=4] {'ctx'}, use_global_device_ids=true, to_apply=%region_10.11 | all-reduce | flops 4 | bytes 32 | tf_op jit(solution)/shard_map/psum | solution.py:106
  418.3 2.3 multiply_reduce_fusion
  423.8 9.0 %psum.15 = f32[]{:T(128)} all-reduce(f32[]{:T(128)S(6)} %select_n.32), channel_id=1, replica_groups=mesh['ctx'=64,'dp'=4] {'dp'}, use_global_device_ids=true, to_apply=%region_14.15 | all-reduce | flops 1 | bytes 8 | tf_op jit(solution)/shard_map/psum | solution.py:108
  432.7 1.7 fusion.3
  435.0 1.2 copy-done.6
  436.1 1.5 fusion
  437.6 2.4 copy.69
  440.6 2.6 convolution_bitcast_fusion.1
  443.7 78.9 %all-gather.11.cloned.1.call-done = bf16[128,4,128,128]{3,2,1,0:T(8,128)(2,1)} async-done(((bf16[2,4,128,128]{3,2,1,0:T(8,128)(2,1)}), bf16[128,4,128,128]{3,2,1,0:T(8,128)(2,1)}) %all-gather.11.cloned.1.call-update) | async-done | bytes 16777232 | tf_op jit(solution)/shard_map/all_gather | solution.py:18
  522.6 68.1 %while.34 = (s32[]{:T(128)}, f32[2,4,128,128]{3,2,1,0:T(8,128)S(1)}, s32[]{:T(128)}, bf16[64,2,4,128,128]{4,3,2,1,0:T(8,128)(2,1)}, s32[]{:T(128)}, /*index=5*/s32[]{:T(128)}, s32[]{:T(128)}, s32[]{:T(128)}) while((s32[]{:T(128)}, f32[2,4,128,128]{3,2,1,0:T(8,128)S(1)}, s32[]{:T(128)}, bf16[64,2,4,128,128]{4,3,2,1,0:T(8,128)(2,1)}, ...), condition=%wide.region_13.14_spmd, body=%wide.region_12.13_spmd.sunk | while | flops 262150 | bytes 1310855 | solution.py:25
  522.6 1.1 convert_add_fusion.8
  (133 shorter events, 80.1 us)
Async XLA Ops:
  7.2 3.3 copy-start.16
  7.2 3.4 copy-start.13
  7.2 108.1 %all-gather.7.cloned.1.call-start = ((), (), s32[]{:S(2)}) async-start(), calls=%async_computation | async-start | bytes 17039360 | tf_op jit(solution)/shard_map/all_gather | solution.py:18
  8.3 4.2 copy-start.12
  10.4 205.0 %all-gather.9.cloned.1.call-start = ((), (), s32[]{:S(2)}) async-start(), calls=%async_computation.1 | async-start | bytes 17039360 | tf_op jit(solution)/shard_map/all_gather | solution.py:18
  11.7 510.8 %all-gather.11.cloned.1.call-start = ((), (), s32[]{:S(2)}) async-start(), calls=%async_computation.2 | async-start | bytes 17039360 | tf_op jit(solution)/shard_map/all_gather | solution.py:18
  13.3 103.2 %copy-start.1 = (bf16[2,128,4,4,128]{4,3,2,1,0:T(4,128)(2,1)}, bf16[2,128,4,4,128]{4,3,2,1,0:T(4,128)(2,1)S(1)}, u32[]{:S(2)}) copy-start(bf16[2,128,4,4,128]{4,3,2,1,0:T(4,128)(2,1)S(1)} %reshape.126) | copy-start | bytes 3145732
  13.5 5.1 copy-start.14
  15.5 201.0 %copy-start.4 = (bf16[2,128,4,4,128]{4,3,2,1,0:T(4,128)(2,1)}, bf16[2,128,4,4,128]{4,3,2,1,0:T(4,128)(2,1)S(1)}, u32[]{:S(2)}) copy-start(bf16[2,128,4,4,128]{4,3,2,1,0:T(4,128)(2,1)S(1)} %reshape.129) | copy-start | bytes 3145732
  216.6 1.8 copy-start.7
  216.6 2.6 copy-start.10
  223.8 2.8 copy-start.17
  418.3 2.3 copy-start
  420.6 1.6 copy-start.2
  421.3 1.0 copy-start.5
  422.7 11.8 %copy-start.15 = (bf16[2,128,4,128,1]{1,3,4,2,0:T(8,128)(2,1)S(1)}, bf16[2,128,4,128,1]{1,3,4,2,0:T(8,128)(2,1)}, u32[]{:S(2)}) copy-start(bf16[2,128,4,128,1]{1,3,4,2,0:T(8,128)(2,1)} %copy-done.14) | copy-start | bytes 786436
  434.5 3.1 copy-start.8
  434.5 1.6 copy-start.6
  437.6 5.6 copy-start.3
  440.6 2.6 copy-start.9
  522.6 68.1 %copy-start.11 = (f32[2,4,128,128]{3,2,1,0:T(8,128)S(1)}, f32[2,4,128,128]{3,2,1,0:T(8,128)}, u32[]{:S(2)}) copy-start(f32[2,4,128,128]{3,2,1,0:T(8,128)} %convolution_bitcast_fusion.1) | copy-start | bytes 1572868
Sparse Core Ops, SparseCore 0:
  11.4 103.9 all-gather.6
  118.7 96.7 all-gather.8
  423.7 98.8 all-gather.10
where the time goes:
time: 605 us; the launch traced here: 601 us
  waiting for transfers between devices  271 us (45%)
  blocking collectives  197 us (33%)
  other arithmetic  74.6 us (12%)
  matrix products  19.5 us (3%)
  between operations  18.7 us (3%)
  local copies, waits for them, and re-layouts  17.8 us (3%)
    all_gather x3, waiting for transfers between devices, carried_in(): gathered = lax.all_gather(x.astype(jnp.bfloat16), axis)  271 us
    psum x1, blocking collectives, shards(): totals = lax.psum(sums, 'ctx')  188 us
    add x64, other arithmetic, add_states(): return earlier + following  68.5 us
  transfers between devices with their start and end apart: 3, of which 3 were waited for; matrix products, arithmetic and copies ran while one was open for 4% of the time, Pallas kernels for 0%

commit v1 on v0

--- a/solution.py
+++ b/solution.py
@@ -103,7 +103,8 @@
     sums = jnp.stack(
         [jnp.sum(mask_rows * policy_tokens, axis=1), jnp.sum(mask_rows * reference_tokens, axis=1)]
     )
-    totals = lax.psum(sums, "ctx")
+    pieces = lax.all_gather(sums, "ctx", axis=0, tiled=False)
+    totals = pieces.sum(axis=0)
     delta = totals[0, 0] - totals[0, 1] - (totals[1, 0] - totals[1, 1])
     pair_loss = lax.psum(jax.nn.softplus(-dpo_beta * delta), "dp") / lax.axis_size("dp")
     scale = math.sqrt(HEADS * D_HEAD * block_rows * lax.axis_size("ctx"))

time: 605 us -> 522 us (0.86)
  blocking collectives: 197 us -> 117 us
    psum x1 -> x0, blocking collectives: 188 us -> none  [shards(): totals = lax.psum(sums, 'ctx')]
    all_gather x0 -> x1, blocking collectives: none -> 108 us  [shards(): pieces = lax.all_gather(sums, 'ctx', axis=0, tiled=False)]
where the time goes in v1:
time: 522 us; the launch traced here: 517 us
  waiting for transfers between devices  268 us (51%)
  blocking collectives  117 us (22%)
  other arithmetic  74.6 us (14%)
  matrix products  19.5 us (4%)
  between operations  18.6 us (4%)
  local copies, waits for them, and re-layouts  17.8 us (3%)
    all_gather x3, waiting for transfers between devices, carried_in(): gathered = lax.all_gather(x.astype(jnp.bfloat16), axis)  268 us
    all_gather x1, blocking collectives, shards(): pieces = lax.all_gather(sums, 'ctx', axis=0, tiled=False)  108 us
    add x64, other arithmetic, add_states(): return earlier + following  68.5 us
  transfers between devices with their start and end apart: 3, of which 3 were waited for; matrix products, arithmetic and copies ran while one was open for 4% of the time, Pallas kernels for 0%

profile of v1, /device:TPU:1, one launch (start us, length us, event | category | flops | bytes accessed | tf_op | source)
XLA Modules:
  0.0 517.1 jit_solution(17892208404402661106)
XLA Ops:
  8.3 1.1 reshape.127
  13.5 2.0 reshape.129
  15.5 3.0 copy.51
  18.5 1.5 fusion.2
  20.1 95.2 %all-gather.9.cloned.1.call-done = bf16[128,4,128,128]{3,2,1,0:T(8,128)(2,1)} async-done(((bf16[2,4,128,128]{3,2,1,0:T(8,128)(2,1)}), bf16[128,4,128,128]{3,2,1,0:T(8,128)(2,1)}) %all-gather.9.cloned.1.call-update) | async-done | bytes 16777232 | tf_op jit(solution)/shard_map/all_gather | solution.py:18
  115.3 1.1 while.32
  115.4 1.1 convert_add_fusion.6
  116.5 1.8 fusion.18
  118.3 97.1 %all-gather.11.cloned.1.call-done = bf16[128,4,128,128]{3,2,1,0:T(8,128)(2,1)} async-done(((bf16[2,4,128,128]{3,2,1,0:T(8,128)(2,1)}), bf16[128,4,128,128]{3,2,1,0:T(8,128)(2,1)}) %all-gather.11.cloned.1.call-update) | async-done | bytes 16777232 | tf_op jit(solution)/shard_map/all_gather | solution.py:18
  215.4 1.1 while.33
  216.6 1.8 fusion.13
  219.7 4.1 multiply_reduce_fusion.2
  223.8 2.8 multiply_reduce_fusion.3
  226.8 107.8 %all-gather.4 = f32[64,2,2]{2,1,0:T(2,128)S(1)} all-gather(f32[1,2,2]{2,1,0:T(2,128)S(1)} %maximum_bitcast_fusion), channel_id=4, replica_groups=mesh['ctx'=64,'dp'=4] {'ctx'}, dimensions={0}, use_global_device_ids=true | all-gather | bytes 1040 | tf_op jit(solution)/shard_map/all_gather | solution.py:106
  338.1 2.3 multiply_reduce_fusion
  343.5 9.0 %psum.7 = f32[]{:T(128)} all-reduce(f32[]{:T(128)S(6)} %select_n.32), channel_id=1, replica_groups=mesh['ctx'=64,'dp'=4] {'dp'}, use_global_device_ids=true, to_apply=%region_14.15 | all-reduce | flops 1 | bytes 8 | tf_op jit(solution)/shard_map/psum | solution.py:109
  352.5 1.7 fusion.3
  354.7 1.2 copy-done.6
  355.9 1.5 fusion
  357.3 2.4 copy.69
  360.4 2.6 convolution_bitcast_fusion.1
  363.4 75.6 %all-gather.13.cloned.1.call-done = bf16[128,4,128,128]{3,2,1,0:T(8,128)(2,1)} async-done(((bf16[2,4,128,128]{3,2,1,0:T(8,128)(2,1)}), bf16[128,4,128,128]{3,2,1,0:T(8,128)(2,1)}) %all-gather.13.cloned.1.call-update) | async-done | bytes 16777232 | tf_op jit(solution)/shard_map/all_gather | solution.py:18
  439.1 68.1 %while.34 = (s32[]{:T(128)}, f32[2,4,128,128]{3,2,1,0:T(8,128)S(1)}, s32[]{:T(128)}, bf16[64,2,4,128,128]{4,3,2,1,0:T(8,128)(2,1)}, s32[]{:T(128)}, /*index=5*/s32[]{:T(128)}, s32[]{:T(128)}, s32[]{:T(128)}) while((s32[]{:T(128)}, f32[2,4,128,128]{3,2,1,0:T(8,128)S(1)}, s32[]{:T(128)}, bf16[64,2,4,128,128]{4,3,2,1,0:T(8,128)(2,1)}, ...), condition=%wide.region_13.14_spmd, body=%wide.region_12.13_spmd.sunk | while | flops 262150 | bytes 1310855 | solution.py:25
  439.1 1.1 convert_add_fusion.8
  (134 shorter events, 80.1 us)
Async XLA Ops:
  7.2 3.3 copy-start.16
  7.2 3.4 copy-start.13
  7.2 108.1 %all-gather.9.cloned.1.call-start = ((), (), s32[]{:S(2)}) async-start(), calls=%async_computation | async-start | bytes 17039360 | tf_op jit(solution)/shard_map/all_gather | solution.py:18
  8.3 4.2 copy-start.12
  10.4 205.0 %all-gather.11.cloned.1.call-start = ((), (), s32[]{:S(2)}) async-start(), calls=%async_computation.1 | async-start | bytes 17039360 | tf_op jit(solution)/shard_map/all_gather | solution.py:18
  11.7 427.3 %all-gather.13.cloned.1.call-start = ((), (), s32[]{:S(2)}) async-start(), calls=%async_computation.2 | async-start | bytes 17039360 | tf_op jit(solution)/shard_map/all_gather | solution.py:18
  13.3 103.2 %copy-start.1 = (bf16[2,128,4,4,128]{4,3,2,1,0:T(4,128)(2,1)}, bf16[2,128,4,4,128]{4,3,2,1,0:T(4,128)(2,1)S(1)}, u32[]{:S(2)}) copy-start(bf16[2,128,4,4,128]{4,3,2,1,0:T(4,128)(2,1)S(1)} %reshape.126) | copy-start | bytes 3145732
  13.5 5.1 copy-start.14
  15.5 201.0 %copy-start.4 = (bf16[2,128,4,4,128]{4,3,2,1,0:T(4,128)(2,1)}, bf16[2,128,4,4,128]{4,3,2,1,0:T(4,128)(2,1)S(1)}, u32[]{:S(2)}) copy-start(bf16[2,128,4,4,128]{4,3,2,1,0:T(4,128)(2,1)S(1)} %reshape.129) | copy-start | bytes 3145732
  216.6 1.8 copy-start.7
  216.6 2.6 copy-start.10
  223.8 2.8 copy-start.17
  338.1 2.3 copy-start
  340.4 1.6 copy-start.2
  341.0 1.0 copy-start.5
  342.4 11.8 %copy-start.15 = (bf16[2,128,4,128,1]{1,3,4,2,0:T(8,128)(2,1)S(1)}, bf16[2,128,4,128,1]{1,3,4,2,0:T(8,128)(2,1)}, u32[]{:S(2)}) copy-start(bf16[2,128,4,128,1]{1,3,4,2,0:T(8,128)(2,1)} %copy-done.14) | copy-start | bytes 786436
  354.2 3.1 copy-start.8
  354.3 1.6 copy-start.6
  357.3 5.6 %copy-start.3 = (bf16[2,128,4,4,128]{4,3,2,1,0:T(4,128)(2,1)S(1)}, bf16[2,128,4,4,128]{4,3,2,1,0:T(4,128)(2,1)}, u32[]{:S(2)}) copy-start(bf16[2,128,4,4,128]{4,3,2,1,0:T(4,128)(2,1)} %copy-done.1) | copy-start | bytes 3145732
  360.3 2.6 copy-start.9
  439.0 68.1 %copy-start.11 = (f32[2,4,128,128]{3,2,1,0:T(8,128)S(1)}, f32[2,4,128,128]{3,2,1,0:T(8,128)}, u32[]{:S(2)}) copy-start(f32[2,4,128,128]{3,2,1,0:T(8,128)} %convolution_bitcast_fusion.1) | copy-start | bytes 1572868
Sparse Core Ops, SparseCore 0:
  11.4 103.9 all-gather.8
  118.7 96.7 all-gather.10
  343.4 95.5 all-gather.12
